TPU v7x, 128 devices: a whole 4x4x4 slice. The times are simulated.
128 devices in a mesh: section: 8 (over y, core), expert: 16 (over x, z).
Axes of the slice: x: 4, y: 4, z: 4, core: 2. Of those that a mesh axis runs over, the one named last changes fastest.
Arguments:
- section_input: bfloat16 [8, 2048, 2880], P('section', 'expert'), may hold values from -6 to 6
- attention_gain: float32 [8, 2880], P('section'), may hold values from 0.1 to 1.9
- query_key_value_weight: bfloat16 [8, 2880, 2560], P('section', 'expert'), may hold values from -0.109375 to 0.109375
- qkv_bias: float32 [8, 2560], P('section'), may hold values from -3 to 8
- out_weight: bfloat16 [8, 2048, 2880], P('section'), may hold values from -0.125 to 0.125
- out_bias: float32 [8, 2880], P('section'), may hold values from -3 to 3
- attention_sink_logits: float32 [8, 32], P('section'), may hold values from -1 to 250
- expert_gain: float32 [8, 2880], P('section'), may hold values from 0.1 to 1.9
- gate_up_weight: bfloat16 [8, 16, 2880, 1440], P('section', 'expert'), may hold values from -0.109375 to 0.109375
- down_weight: bfloat16 [8, 16, 720, 2880], P('section', 'expert'), may hold values from -0.15625 to 0.15625
- expert_ids: int32 [8, 2048, 4], P('section', 'expert'), may hold values from 0 to 7, all different within a row; in each aligned block of 128 rows (0 to 127, 128 to 255, ..., all dimensions but the last counted through in order) at most 80 rows name the same one
- gate_logits: float32 [8, 2048, 4], P('section', 'expert'), may hold values from -8 to 204
- placement: int32 [8, 8], P('section'), may hold values from 0 to 7, each once within a row
Outputs:
- section_output: bfloat16 [8, 2048, 2880], P('section', 'expert')
Inputs may be any that keep to these rules, and one draw needn't show every extreme that they name: `expert_ids`: within each section, among the 128 tokens of one device no expert is named more than 80 times, a bound that some block reaches. `placement`: each row names every expert once.
All inputs are finite; a program needn't handle non-finite values.
Results may differ from a plain program's by a relative error of at most 0.018.
Values may be sent and summed in bfloat16 or wider, within the bound.
A program may use at most 128 MiB of HBM per device.

v0:
```python
import jax
import jax.numpy as jnp
from jax import lax
from jax.sharding import PartitionSpec as P

HEAD_DIM = 64
QUERY_HEADS = 32
KEY_VALUE_HEADS = 4
WINDOW_TOKENS = 128
TOP = 4


def from_behind(x, axis, by):
    size = lax.axis_size(axis)
    pairs = [(i, i + by) for i in range(size) if 0 <= i + by < size]
    return lax.ppermute(x, axis, pairs)


def passed_along(x, axis, by):
    size = lax.axis_size(axis)
    return lax.ppermute(x, axis, [(i, (i + by) % size) for i in range(size)])


def normed(vector, gain_row):
    as_float = vector.astype(jnp.float32)
    inverse_rms = lax.rsqrt(jnp.mean(as_float * as_float, axis=-1, keepdims=True) + 1e-05)
    return (as_float * inverse_rms * gain_row).astype(jnp.bfloat16)


def swiglu(hidden):
    half_cols = hidden.shape[1] // 2
    gate_part = hidden[:, :half_cols]
    up_part = hidden[:, half_cols:]
    return ((up_part + 1.0) * gate_part * jax.nn.sigmoid(1.702 * gate_part)).astype(jnp.bfloat16)


def shards(
    section_input,
    attention_gain,
    query_key_value_weight,
    qkv_bias,
    out_weight,
    out_bias,
    attention_sink_logits,
    expert_gain,
    gate_up_weight,
    down_weight,
    expert_ids,
    gate_logits,
    placement,
):
    count_of_rows = section_input.shape[1]
    model_width = section_input.shape[2]
    experts_count = placement.shape[1]
    slot_count = 2 * min(count_of_rows // 2, count_of_rows * TOP * 5 // (8 * experts_count))
    offset = lax.axis_index("expert") * count_of_rows
    query_group_width = QUERY_HEADS // KEY_VALUE_HEADS
    tile_gu = gate_up_weight[0, 0]
    tile_down = down_weight[0, 0]
    state = section_input[0]
    normed_in = normed(state, attention_gain[0])
    projected_rows = (
        jnp.dot(
            normed_in,
            lax.all_gather(query_key_value_weight[0], "expert", axis=0, tiled=True),
            preferred_element_type=jnp.float32,
        )
        + qkv_bias[0]
    ).astype(jnp.bfloat16)
    query_rows = projected_rows[:, : QUERY_HEADS * HEAD_DIM].reshape(
        count_of_rows, KEY_VALUE_HEADS, query_group_width, HEAD_DIM
    )
    key_value = projected_rows[:, QUERY_HEADS * HEAD_DIM :]
    rim_rows = from_behind(key_value, "expert", 1)
    rows_in_window = jnp.concatenate([rim_rows, key_value], 0)
    key_row_slice = rows_in_window[:, : KEY_VALUE_HEADS * HEAD_DIM].reshape(
        WINDOW_TOKENS + count_of_rows, KEY_VALUE_HEADS, HEAD_DIM
    )
    value_row_slice = rows_in_window[:, KEY_VALUE_HEADS * HEAD_DIM :].reshape(
        WINDOW_TOKENS + count_of_rows, KEY_VALUE_HEADS, HEAD_DIM
    )
    scores = (
        jnp.einsum("ikgd,jkd->kgij", query_rows, key_row_slice, preferred_element_type=jnp.float32)
        * 0.125
    )
    query_pos = offset + jnp.arange(count_of_rows, dtype=jnp.int32)
    key_pos = offset - WINDOW_TOKENS + jnp.arange(WINDOW_TOKENS + count_of_rows, dtype=jnp.int32)
    distance = query_pos[:, None] - key_pos[None, :]
    inside = (distance >= 0) & (distance < WINDOW_TOKENS) & (key_pos >= 0)[None, :]
    head_sink_logit = attention_sink_logits[0].reshape(KEY_VALUE_HEADS, query_group_width)[
        :, :, None
    ]
    masked = jnp.where(inside, scores, -1e30)
    peak = jnp.maximum(jnp.max(masked, axis=-1), head_sink_logit)
    numer = jnp.where(inside, jnp.exp(masked - peak[..., None]), 0.0)
    denominator = jnp.sum(numer, axis=-1) + jnp.exp(head_sink_logit - peak)
    attention = (numer / denominator[..., None]).astype(jnp.bfloat16)
    mixed = jnp.einsum(
        "kgij,jkd->ikgd", attention, value_row_slice, preferred_element_type=jnp.float32
    )
    attended = mixed.astype(jnp.bfloat16).reshape(count_of_rows, QUERY_HEADS * HEAD_DIM)
    residual = (
        state.astype(jnp.float32)
        + jnp.dot(attended, out_weight[0], preferred_element_type=jnp.float32)
        + out_bias[0]
    ).astype(jnp.bfloat16)
    normed_mid = normed(residual, expert_gain[0])
    flat_ids = expert_ids[0].reshape(-1)
    expert_range = jnp.arange(experts_count, dtype=jnp.int32)
    one_hot = (flat_ids[:, None] == expert_range[None, :]).astype(jnp.int32)
    slot_of = jnp.sum((jnp.cumsum(one_hot, axis=0) - 1) * one_hot, axis=-1)
    token_of = jnp.arange(count_of_rows * TOP, dtype=jnp.int32) // TOP
    source_rows = (
        jnp.full((experts_count * slot_count,), -1, jnp.int32)
        .at[flat_ids * slot_count + slot_of]
        .set(token_of)
    )
    valid_rows = (source_rows >= 0)[:, None].astype(jnp.bfloat16)
    gathered = jnp.take(normed_mid, jnp.maximum(source_rows, 0), axis=0) * valid_rows
    by_expert = gathered.reshape(experts_count, slot_count, model_width)
    holders = placement[0]
    by_pair = jnp.take(by_expert, holders, axis=0)
    matches = (holders[:, None] == expert_range[None, :]).astype(jnp.int32)
    holder_of = jnp.sum(expert_range[:, None] * matches, axis=0)
    outgoing = jnp.repeat(by_pair, 2, axis=0)
    rows_in = lax.all_to_all(outgoing, "expert", split_axis=0, concat_axis=0, tiled=True)
    in_shape = rows_in.shape
    hidden = jnp.dot(rows_in.reshape(-1, model_width), tile_gu, preferred_element_type=jnp.float32)
    returned = lax.all_to_all(
        jnp.dot(swiglu(hidden), tile_down, preferred_element_type=jnp.float32)
        .astype(jnp.bfloat16)
        .reshape(in_shape),
        "expert",
        split_axis=0,
        concat_axis=0,
        tiled=True,
    )
    paired = returned.astype(jnp.float32).reshape(experts_count, 2, slot_count, model_width)
    summed = (
        (paired[:, 0] + paired[:, 1])
        .astype(jnp.bfloat16)
        .reshape(experts_count * slot_count, model_width)
    )
    picked = jnp.take(summed, holder_of[flat_ids] * slot_count + slot_of, axis=0).reshape(
        count_of_rows, TOP, model_width
    )
    picked = lax.optimization_barrier(picked).astype(jnp.float32)
    gate_weights = jax.nn.softmax(gate_logits[0], axis=-1)
    fresh = (
        residual.astype(jnp.float32) + jnp.sum(picked * gate_weights[..., None], axis=1)
    ).astype(jnp.bfloat16)
    moved = passed_along(fresh, "section", 1)
    return moved[None]


def solution(mesh):
    return jax.shard_map(
        shards,
        mesh=mesh,
        in_specs=(
            P("section", "expert", None),
            P("section", None),
            P("section", "expert", None),
            P("section", None),
            P("section", None, None),
            P("section", None),
            P("section", None),
            P("section", None),
            P("section", "expert", None, None),
            P("section", "expert", None, None),
            P("section", "expert", None),
            P("section", "expert", None),
            P("section", None),
        ),
        out_specs=P("section", "expert", None),
        check_vma=False,
    )
```

profile of v0, /device:TPU:0, one launch (start us, length us, event | category | flops | bytes accessed | tf_op | source)
XLA Modules:
  0.0 547.5 jit_solution(6834803989660928297)
XLA Ops:
  6.6 4.0 copy.62
  13.5 4.4 compare_select_fusion.4
  18.5 2.4 scatter_custom_fusion
  21.6 168.0 %all-gather.3.cloned.1.call-done = bf16[1,2880,2560]{2,0,1:T(2,128)(2,1)} async-done(((bf16[1,180,2560]{2,0,1:T(2,128)(2,1)}), bf16[1,2880,2560]{2,0,1:T(2,128)(2,1)}) %all-gather.3.cloned.1.call-update) | async-done | bytes 14745616 | tf_op jit(solution)/shard_map/all_gather | solution.py:65
  189.7 15.2 %fusion.17 = bf16[128,2560]{1,0:T(8,128)(2,1)S(1)} fusion(bf16[1,2880,2560]{2,0,1:T(2,128)(2,1)} %all-gather.3.cloned.1.call-done, bf16[1,128,2880]{1,2,0:T(8,128)(2,1)S(1)} %copy-done.2, f32[2880]{0:T(1024)S(1)} %reduce.1, f32[128]{0:T(128)S(1)} %add_rsqrt_fusion.1, f32[2560]{0:T(1024)S(1)} %reduce.2), kind=kOutput, calls=%fused_computation.29 | convolution fusion | flops 1889566720 | bytes 16160512 | tf_op jit(solution)/shard_map/dot_general | solution.py:63
  204.9 3.7 collective-permute-start
  216.6 3.3 multiply_reduce_fusion.1
  221.8 4.6 gather_fusion
  226.4 4.5 select_multiply_fusion
  230.9 4.9 gather_fusion.1
  235.7 2.5 broadcast_select_fusion
  238.8 93.2 %all_to_all.10 = bf16[16,80,2880]{2,1,0:T(8,128)(2,1)S(1)} all-to-all(bf16[16,80,2880]{2,1,0:T(8,128)(2,1)S(1)} %bitcast.119), channel_id=1, replica_groups=mesh['section'=8,'expert'=16] {'expert'}, dimensions={0} | all-to-all | bytes 14745600 | tf_op jit(solution)/shard_map/all_to_all | solution.py:126
  332.0 15.5 %fusion.5 = f32[1280,1440]{0,1:T(8,128)} fusion(bf16[1280,2880]{1,0:T(8,128)(2,1)S(1)} %bitcast.121, bf16[1,1,2880,1440]{2,3,1,0:T(8,128)(2,1)} %param.21), kind=kOutput, calls=%fused_computation.10 | convolution fusion | flops 10616832000 | bytes 23040000 | tf_op jit(solution)/shard_map/dot_general | solution.py:128
  347.4 11.9 %convolution_convert_fusion = bf16[1280,2880]{0,1:T(8,128)(2,1)} fusion(bf16[1,1,720,2880]{3,2,1,0:T(8,128)(2,1)S(1)} %bitcast.134, f32[1280,1440]{0,1:T(8,128)} %fusion.5), kind=kOutput, calls=%fused_computation.9 | convolution fusion | flops 5319475200 | bytes 18892800 | tf_op jit(solution)/shard_map/dot_general | solution.py:130
  359.4 10.4 %copy.71 = bf16[1280,2880]{1,0:T(8,128)(2,1)} copy(bf16[1280,2880]{0,1:T(8,128)(2,1)} %convolution_convert_fusion) | data formatting | bytes 14745600 | tf_op jit(solution)/shard_map/convert_element_type | solution.py:131
  369.8 4.8 all-to-all-start.1
  375.0 112.0 %all-to-all-done.1 = bf16[16,80,2880]{2,1,0:T(8,128)(2,1)} async-done(((bf16[16,80,2880]{2,1,0:T(8,128)(2,1)}), bf16[16,80,2880]{2,1,0:T(8,128)(2,1)}, u32[]{:S(2)}, u32[]{:S(2)}) %all-to-all-start.1) | async-done | bytes 7372832 | tf_op jit(solution)/shard_map/all_to_all | solution.py:129
  487.0 9.5 %convert.4 = f32[8,2,80,2880]{3,2,1,0:T(8,128)} convert(bf16[8,2,80,2880]{3,2,1,0:T(8,128)(2,1)} %bitcast.36) | non-fusion elementwise | flops 3686400 | bytes 22118400 | tf_op jit(solution)/shard_map/reshape | solution.py:138
  496.5 7.8 %fusion.8 = bf16[8,1,80,2880]{3,2,0,1:T(8,128)(2,1)} fusion(f32[8,2,80,2880]{3,2,1,0:T(8,128)} %convert.4), kind=kLoop, calls=%fused_computation.14 | loop fusion | flops 3686400 | bytes 18432000 | tf_op jit(solution)/shard_map/convert_element_type | solution.py:141
  504.3 9.3 %gather_fusion.2 = bf16[512,2880]{1,0:T(8,128)(2,1)} fusion(bf16[640,2880]{1,0:T(8,128)(2,1)} %bitcast.117, s32[1024]{0:T(1024)S(1)} %pad_clamp_fusion), kind=kCustom, calls=%fused_computation.2 | custom fusion | bytes 5900288 | tf_op jit(solution)/shard_map/jit(_take)/gather | solution.py:144
  513.6 4.9 gather.24
  519.9 4.5 multiply_reduce_fusion
  524.4 1.6 copy.75
  527.5 12.1 %collective-permute-done.1 = bf16[128,2880]{0,1:T(8,128)(2,1)S(1)} collective-permute-done((bf16[128,2880]{0,1:T(8,128)(2,1)S(1)}, bf16[128,2880]{0,1:T(8,128)(2,1)S(1)}, u32[]{:S(2)}, u32[]{:S(2)}) %collective-permute-start.1) | collective-permute-done | bytes 737312 | tf_op jit(solution)/shard_map/ppermute | solution.py:21
  (100 shorter events, 18.6 us)
Async XLA Ops:
  6.5 4.0 copy-start.8
  6.5 4.5 copy-start.4
  6.5 4.5 copy-start.7
  6.5 6.0 %copy-start.9 = (s32[1,8]{1,0:T(1,128)S(1)}, s32[1,8]{1,0:T(1,128)}, u32[]{:S(2)}) copy-start(s32[1,8]{1,0:T(1,128)} %param.25) | copy-start | bytes 100
  6.5 14.5 %copy-start.2 = (bf16[1,128,2880]{1,2,0:T(8,128)(2,1)S(1)}, bf16[1,128,2880]{1,2,0:T(8,128)(2,1)}, u32[]{:S(2)}) copy-start(bf16[1,128,2880]{1,2,0:T(8,128)(2,1)} %param.13) | copy-start | bytes 2211844
  6.5 183.1 %all-gather.3.cloned.1.call-start = ((), (), s32[]{:S(2)}) async-start(), calls=%async_computation.2 | async-start | bytes 31334400 | tf_op jit(solution)/shard_map/all_gather | solution.py:65
  21.6 187.0 %copy-start.5 = (f32[1,2880]{1,0:T(1,128)S(1)}, f32[1,2880]{1,0:T(1,128)}, u32[]{:S(2)}) copy-start(f32[1,2880]{1,0:T(1,128)} %param.18) | copy-start | bytes 34564
  21.6 187.6 %copy-start.10 = (f32[1,32]{1,0:T(1,128)S(1)}, f32[1,32]{1,0:T(1,128)}, u32[]{:S(2)}) copy-start(f32[1,32]{1,0:T(1,128)} %param.19) | copy-start | bytes 388
  21.6 188.3 %copy-start.6 = (f32[1,2880]{1,0:T(1,128)S(1)}, f32[1,2880]{1,0:T(1,128)}, u32[]{:S(2)}) copy-start(f32[1,2880]{1,0:T(1,128)} %param.20) | copy-start | bytes 34564
  204.9 6.0 %collective-permute-start = (bf16[128,512]{1,0:T(8,128)(2,1)S(1)}, bf16[128,512]{1,0:T(8,128)(2,1)S(1)}, u32[]{:S(2)}, u32[]{:S(2)}) collective-permute-start(bf16[128,512]{1,0:T(8,128)(2,1)S(1)} %slice.55), channel_id=1, source_target_pairs={{0,1},{1,2},{2,3},{3,4},{4,5},{5,6},{6,7},{7,8},{8,9},{9,10},{10,1... | collective-permute-start | bytes 393224 | tf_op jit(solution)/shard_map/ppermute | solution.py:16
  211.9 2.5 slice-start
  213.1 2.5 slice-start.1
  213.1 3.5 slice-start.2
  219.9 1.2 copy-start
  238.8 108.7 %slice-start.3 = ((s8[4239360]{0:T(1024)(128)(4,1)}), s8[45056]{0:T(1024)(128)(4,1)S(1)}, s32[]{:S(2)}) async-start(s8[4239360]{0:T(1024)(128)(4,1)} %bitcast.133), calls=%async_computation.6 | async-start | bytes 90112
  332.0 15.5 %slice-start.4 = ((s8[4239360]{0:T(1024)(128)(4,1)}), s8[4194304]{0:T(1024)(128)(4,1)S(1)}, s32[]{:S(2)}) async-start(s8[4239360]{0:T(1024)(128)(4,1)} %bitcast.133), calls=%async_computation.7 | async-start | bytes 8388608
  369.8 5.0 copy-start.3
  369.8 117.2 %all-to-all-start.1 = ((bf16[16,80,2880]{2,1,0:T(8,128)(2,1)}), bf16[16,80,2880]{2,1,0:T(8,128)(2,1)}, u32[]{:S(2)}, u32[]{:S(2)}) async-start(bf16[16,80,2880]{2,1,0:T(8,128)(2,1)} %bitcast.118), calls=%async_computation.1 | async-start | bytes 15073280 | tf_op jit(solution)/shard_map/all_to_all | solution.py:129
  519.9 6.1 %copy-start.1 = (f32[128,2880]{0,1:T(8,128)S(1)}, f32[128,2880]{0,1:T(8,128)}, u32[]{:S(2)}) copy-start(f32[128,2880]{0,1:T(8,128)} %copy-done) | copy-start | bytes 4423684
  527.5 12.1 %collective-permute-start.1 = (bf16[128,2880]{0,1:T(8,128)(2,1)S(1)}, bf16[128,2880]{0,1:T(8,128)(2,1)S(1)}, u32[]{:S(2)}, u32[]{:S(2)}) collective-permute-start(bf16[128,2880]{0,1:T(8,128)(2,1)S(1)} %add_convert_fusion), channel_id=1, source_target_pairs={{0,16},{16,32},{32,48},{48,64},{64,80},{80,96},{96,112},{112,0},{1... | collective-permute-start | bytes 2211848 | tf_op jit(solution)/shard_map/ppermute | solution.py:21
Sparse Core Ops, SparseCore 0:
  10.7 178.9 all-gather.2
where the time goes:
time: 555 us; the launch traced here: 548 us
  waiting for transfers between devices  293 us (53%)
  blocking collectives  93.2 us (17%)
  local copies, waits for them, and re-layouts  50 us (9%)
  matrix products  47.9 us (9%)
  other arithmetic  41.3 us (7%)
  between operations  14.1 us (3%)
  starting transfers between devices  8.6 us (2%)
    all_gather x1, waiting for transfers between devices, shards(): lax.all_gather(query_key_value_weight[0], 'expert', axis=0, tiled=True)  168 us
    all_to_all x1, waiting for transfers between devices, shards(): lax.all_to_all(jnp.dot(swiglu(hidden), tile_down, preferred_element_type=...  112 us
    all_to_all x1, blocking collectives, shards(): lax.all_to_all(outgoing, 'expert', split_axis=0, concat_axis=0, tiled=True)  93.2 us
    dot_general x1, matrix products, shards(): jnp.dot(rows_in.reshape(-1, model_width), tile_gu, preferred_element_type...  15.5 us
    dot_general x1, matrix products, shards(): jnp.dot(normed_in, lax.all_gather(query_key_value_weight[0], 'expert', ax...  15.2 us
    gather x2, local copies, waits for them, and re-layouts, shards(): jnp.take(summed, holder_of[flat_ids] * slot_count + slot_of, axis=0)  14.1 us
    ppermute x1, waiting for transfers between devices, passed_along(): return lax.ppermute(x, axis, [(i, (i + by) % size) for i in range(size)])  12.1 us
    dot_general x1, matrix products, shards(): jnp.dot(swiglu(hidden), tile_down, preferred_element_type=jnp.float32)  11.9 us
  transfers between devices with their start and end apart: 4, of which 4 were waited for; matrix products, arithmetic and copies ran while one was open for 2% of the time, Pallas kernels for 0%

commit v1 on v0

--- a/solution.py
+++ b/solution.py
@@ -62,7 +62,12 @@
     projected_rows = (
         jnp.dot(
             normed_in,
-            lax.all_gather(query_key_value_weight[0], "expert", axis=0, tiled=True),
+            jnp.concatenate(
+                lax.all_to_all(
+                    jnp.stack([query_key_value_weight[0]] * lax.axis_size("expert")), "expert", 0, 0
+                ),
+                axis=0,
+            ),
             preferred_element_type=jnp.float32,
         )
         + qkv_bias[0]

time: 555 us -> 616 us (1.11); the launches traced: 548 us -> 615 us
  waiting for transfers between devices: 293 us -> 353 us
  local copies, waits for them, and re-layouts: 50 us -> 66.1 us
  between operations: 14.1 us -> 0.45 us
  starting transfers between devices: 8.6 us -> 21.5 us
  matrix products: 47.9 us -> 40.3 us
    all_to_all x0 -> x1, waiting for transfers between devices: none -> 249 us  [shards(): lax.all_to_all(jnp.stack([query_key_value_weight[0]] * lax.axis_size('exp...]
    all_gather x1 -> x0, waiting for transfers between devices: 168 us -> none  [shards(): lax.all_gather(query_key_value_weight[0], 'expert', axis=0, tiled=True)]
    all_to_all x1, waiting for transfers between devices: 112 us -> 91.4 us  [shards(): lax.all_to_all(jnp.dot(swiglu(hidden), tile_down, preferred_element_type=...]
    reshape x0 -> x1, local copies, waits for them, and re-layouts: none -> 13.5 us  [shards(): jnp.concatenate(lax.all_to_all(jnp.stack([query_key_value_weight[0]] * la...]
    all_to_all x0 -> x1, starting transfers between devices: none -> 8.15 us  [shards(): lax.all_to_all(jnp.stack([query_key_value_weight[0]] * lax.axis_size('exp...]
    dot_general x1, matrix products: 15.2 us -> 7.53 us  [shards(): jnp.dot(normed_in, jnp.concatenate(lax.all_to_all(jnp.stack([query_key_va...]
    another operation x1 -> x2, local copies, waits for them, and re-layouts: 0.01 us -> 6.56 us  [the longest x1 6.56 us: shards(): jnp.stack([query_key_value_weight[0]] * lax.axis_size('expert'))]
where the time goes in v1:
time: 616 us; the launch traced here: 615 us
  waiting for transfers between devices  353 us (57%)
  blocking collectives  92.7 us (15%)
  local copies, waits for them, and re-layouts  66.1 us (11%)
  other arithmetic  41.3 us (7%)
  matrix products  40.3 us (7%)
  starting transfers between devices  21.5 us (3%)
    all_to_all x1, waiting for transfers between devices, shards(): lax.all_to_all(jnp.stack([query_key_value_weight[0]] * lax.axis_size('exp...  249 us
    all_to_all x1, blocking collectives, shards(): lax.all_to_all(outgoing, 'expert', split_axis=0, concat_axis=0, tiled=True)  92.7 us
    all_to_all x1, waiting for transfers between devices, shards(): lax.all_to_all(jnp.dot(swiglu(hidden), tile_down, preferred_element_type=...  91.4 us
    dot_general x1, matrix products, shards(): jnp.dot(rows_in.reshape(-1, model_width), tile_gu, preferred_element_type...  15.5 us
    gather x2, local copies, waits for them, and re-layouts, shards(): jnp.take(summed, holder_of[flat_ids] * slot_count + slot_of, axis=0)  14.2 us
    reshape x1, local copies, waits for them, and re-layouts, shards(): jnp.concatenate(lax.all_to_all(jnp.stack([query_key_value_weight[0]] * la...  13.5 us
  transfers between devices with their start and end apart: 4, of which 4 were waited for; matrix products, arithmetic and copies ran while one was open for 2% of the time, Pallas kernels for 0%

profile of v1, /device:TPU:0, one launch (start us, length us, event | category | flops | bytes accessed | tf_op | source)
XLA Modules:
  0.0 615.0 jit_solution(14002907000038139193)
XLA Ops:
  0.0 6.6 %stack.3 = bf16[16,180,2560]{2,1,0:T(8,128)(2,1)} broadcast(bf16[180,2560]{1,0:T(8,128)(2,1)} %bitcast.121), dimensions={1,2} | broadcast | bytes 15667200 | tf_op jit(solution)/shard_map/stack | solution.py:67
  6.6 8.1 %all-to-all-start = ((bf16[16,180,2560]{2,1,0:T(8,128)(2,1)}), bf16[16,180,2560]{2,1,0:T(8,128)(2,1)}, u32[]{:S(2)}, u32[]{:S(2)}) async-start(bf16[16,180,2560]{2,1,0:T(8,128)(2,1)} %stack.3), calls=%async_computation | async-start | bytes 30146560 | tf_op jit(solution)/shard_map/all_to_all | solution.py:66
  17.6 4.3 compare_select_fusion.4
  25.7 248.9 %all-to-all-done = bf16[16,180,2560]{2,1,0:T(8,128)(2,1)} async-done(((bf16[16,180,2560]{2,1,0:T(8,128)(2,1)}), bf16[16,180,2560]{2,1,0:T(8,128)(2,1)}, u32[]{:S(2)}, u32[]{:S(2)}) %all-to-all-start) | async-done | bytes 14745632 | tf_op jit(solution)/shard_map/all_to_all | solution.py:66
  274.6 13.5 %reshape.297 = bf16[2880,2560]{1,0:T(8,128)(2,1)} reshape(bf16[16,180,2560]{2,1,0:T(8,128)(2,1)} %all-to-all-done) | data formatting | bytes 29491200 | tf_op jit(solution)/shard_map/reshape | solution.py:65
  288.1 7.5 %fusion.11 = bf16[128,2560]{1,0:T(8,128)(2,1)S(1)} fusion(bf16[2880,2560]{1,0:T(8,128)(2,1)} %reshape.297, bf16[1,128,2880]{1,2,0:T(8,128)(2,1)S(1)} %copy-done.2, f32[2880]{0:T(1024)S(1)} %reduce.1, f32[128]{0:T(128)S(1)} %add_rsqrt_fusion.1, f32[2560]{0:T(1024)S(1)} %reduce.2), kind=kOutput, calls=%fused_computation.26 | convolution fusion | flops 1889566720 | bytes 16160512 | tf_op jit(solution)/shard_map/dot_general | solution.py:63
  295.6 8.5 %collective-permute-start = (bf16[128,512]{1,0:T(8,128)(2,1)S(1)}, bf16[128,512]{1,0:T(8,128)(2,1)S(1)}, u32[]{:S(2)}, u32[]{:S(2)}) collective-permute-start(bf16[128,512]{1,0:T(8,128)(2,1)S(1)} %slice.55), channel_id=1, source_target_pairs={{0,1},{1,2},{2,3},{3,4},{4,5},{5,6},{6,7},{7,8},{8,9},{9,10},{10,1... | collective-permute-start | bytes 393224 | tf_op jit(solution)/shard_map/ppermute | solution.py:16
  312.2 3.3 multiply_reduce_fusion.1
  317.5 4.6 gather_fusion
  322.0 4.5 select_multiply_fusion
  326.5 4.9 gather_fusion.1
  331.4 2.5 broadcast_select_fusion
  334.4 92.7 %all_to_all.15 = bf16[16,80,2880]{2,1,0:T(8,128)(2,1)S(1)} all-to-all(bf16[16,80,2880]{2,1,0:T(8,128)(2,1)S(1)} %bitcast.117), channel_id=1, replica_groups=mesh['section'=8,'expert'=16] {'expert'}, dimensions={0} | all-to-all | bytes 14745600 | tf_op jit(solution)/shard_map/all_to_all | solution.py:131
  427.1 15.5 %fusion.2 = f32[1280,1440]{0,1:T(8,128)} fusion(bf16[1280,2880]{1,0:T(8,128)(2,1)S(1)} %bitcast.119, bf16[1,1,2880,1440]{2,3,1,0:T(8,128)(2,1)} %param.21), kind=kOutput, calls=%fused_computation.7 | convolution fusion | flops 10616832000 | bytes 23040000 | tf_op jit(solution)/shard_map/dot_general | solution.py:133
  442.6 11.9 %convolution_convert_fusion = bf16[1280,2880]{0,1:T(8,128)(2,1)} fusion(bf16[1,1,720,2880]{3,2,1,0:T(8,128)(2,1)S(1)} %bitcast.133, f32[1280,1440]{0,1:T(8,128)} %fusion.2), kind=kOutput, calls=%fused_computation.6 | convolution fusion | flops 5319475200 | bytes 18892800 | tf_op jit(solution)/shard_map/dot_general | solution.py:135
  454.5 10.4 %copy.55 = bf16[1280,2880]{1,0:T(8,128)(2,1)} copy(bf16[1280,2880]{0,1:T(8,128)(2,1)} %convolution_convert_fusion) | data formatting | bytes 14745600 | tf_op jit(solution)/shard_map/convert_element_type | solution.py:136
  464.9 4.8 all-to-all-start.2
  470.1 91.4 %all-to-all-done.2 = bf16[16,80,2880]{2,1,0:T(8,128)(2,1)} async-done(((bf16[16,80,2880]{2,1,0:T(8,128)(2,1)}), bf16[16,80,2880]{2,1,0:T(8,128)(2,1)}, u32[]{:S(2)}, u32[]{:S(2)}) %all-to-all-start.2) | async-done | bytes 7372832 | tf_op jit(solution)/shard_map/all_to_all | solution.py:134
  561.5 9.5 %convert.3 = f32[8,2,80,2880]{3,2,1,0:T(8,128)} convert(bf16[8,2,80,2880]{3,2,1,0:T(8,128)(2,1)} %bitcast.37) | non-fusion elementwise | flops 3686400 | bytes 22118400 | tf_op jit(solution)/shard_map/reshape | solution.py:143
  571.1 7.8 %fusion.5 = bf16[8,1,80,2880]{3,2,0,1:T(8,128)(2,1)} fusion(f32[8,2,80,2880]{3,2,1,0:T(8,128)} %convert.3), kind=kLoop, calls=%fused_computation.11 | loop fusion | flops 3686400 | bytes 18432000 | tf_op jit(solution)/shard_map/convert_element_type | solution.py:146
  578.9 9.3 %gather_fusion.2 = bf16[512,2880]{1,0:T(8,128)(2,1)} fusion(bf16[640,2880]{1,0:T(8,128)(2,1)} %bitcast.115, s32[1024]{0:T(1024)S(1)} %pad_clamp_fusion), kind=kCustom, calls=%fused_computation.2 | custom fusion | bytes 5900288 | tf_op jit(solution)/shard_map/jit(_take)/gather | solution.py:149
  588.1 4.9 gather.24
  594.5 4.5 multiply_reduce_fusion
  602.1 12.1 %collective-permute-done.1 = bf16[128,2880]{0,1:T(8,128)(2,1)S(1)} collective-permute-done((bf16[128,2880]{0,1:T(8,128)(2,1)S(1)}, bf16[128,2880]{0,1:T(8,128)(2,1)S(1)}, u32[]{:S(2)}, u32[]{:S(2)}) %collective-permute-start.1) | collective-permute-done | bytes 737312 | tf_op jit(solution)/shard_map/ppermute | solution.py:21
  (100 shorter events, 22.6 us)
Async XLA Ops:
  6.6 8.2 %copy-start.8 = (s32[1,128,4]{1,2,0:T(4,128)S(1)}, s32[1,128,4]{1,2,0:T(4,128)}, u32[]{:S(2)}) copy-start(s32[1,128,4]{1,2,0:T(4,128)} %param.23) | copy-start | bytes 6148
  6.6 8.6 %copy-start.4 = (f32[1,2880]{1,0:T(1,128)S(1)}, f32[1,2880]{1,0:T(1,128)}, u32[]{:S(2)}) copy-start(f32[1,2880]{1,0:T(1,128)} %param.14) | copy-start | bytes 34564
  6.6 8.7 %copy-start.7 = (f32[1,2560]{1,0:T(1,128)S(1)}, f32[1,2560]{1,0:T(1,128)}, u32[]{:S(2)}) copy-start(f32[1,2560]{1,0:T(1,128)} %param.16) | copy-start | bytes 30724
  6.6 10.2 %copy-start.9 = (s32[1,8]{1,0:T(1,128)S(1)}, s32[1,8]{1,0:T(1,128)}, u32[]{:S(2)}) copy-start(s32[1,8]{1,0:T(1,128)} %param.25) | copy-start | bytes 100
  6.6 18.5 %copy-start.2 = (bf16[1,128,2880]{1,2,0:T(8,128)(2,1)S(1)}, bf16[1,128,2880]{1,2,0:T(8,128)(2,1)}, u32[]{:S(2)}) copy-start(bf16[1,128,2880]{1,2,0:T(8,128)(2,1)} %param.13) | copy-start | bytes 2211844
  6.6 268.0 %all-to-all-start = ((bf16[16,180,2560]{2,1,0:T(8,128)(2,1)}), bf16[16,180,2560]{2,1,0:T(8,128)(2,1)}, u32[]{:S(2)}, u32[]{:S(2)}) async-start(bf16[16,180,2560]{2,1,0:T(8,128)(2,1)} %stack.3), calls=%async_computation | async-start | bytes 30146560 | tf_op jit(solution)/shard_map/all_to_all | solution.py:66
  288.1 16.1 %copy-start.5 = (f32[1,2880]{1,0:T(1,128)S(1)}, f32[1,2880]{1,0:T(1,128)}, u32[]{:S(2)}) copy-start(f32[1,2880]{1,0:T(1,128)} %param.18) | copy-start | bytes 34564
  288.1 16.7 %copy-start.10 = (f32[1,32]{1,0:T(1,128)S(1)}, f32[1,32]{1,0:T(1,128)}, u32[]{:S(2)}) copy-start(f32[1,32]{1,0:T(1,128)} %param.19) | copy-start | bytes 388
  288.1 17.4 %copy-start.6 = (f32[1,2880]{1,0:T(1,128)S(1)}, f32[1,2880]{1,0:T(1,128)}, u32[]{:S(2)}) copy-start(f32[1,2880]{1,0:T(1,128)} %param.20) | copy-start | bytes 34564
  295.6 10.8 %collective-permute-start = (bf16[128,512]{1,0:T(8,128)(2,1)S(1)}, bf16[128,512]{1,0:T(8,128)(2,1)S(1)}, u32[]{:S(2)}, u32[]{:S(2)}) collective-permute-start(bf16[128,512]{1,0:T(8,128)(2,1)S(1)} %slice.55), channel_id=1, source_target_pairs={{0,1},{1,2},{2,3},{3,4},{4,5},{5,6},{6,7},{7,8},{8,9},{9,10},{10,1... | collective-permute-start | bytes 393224 | tf_op jit(solution)/shard_map/ppermute | solution.py:16
  307.6 2.5 slice-start
  308.7 2.5 slice-start.1
  308.7 3.5 slice-start.2
  315.5 1.2 copy-start
  334.4 108.2 %slice-start.3 = ((s8[4239360]{0:T(1024)(128)(4,1)}), s8[45056]{0:T(1024)(128)(4,1)S(1)}, s32[]{:S(2)}) async-start(s8[4239360]{0:T(1024)(128)(4,1)} %bitcast.132), calls=%async_computation.6 | async-start | bytes 90112
  427.1 15.5 %slice-start.4 = ((s8[4239360]{0:T(1024)(128)(4,1)}), s8[4194304]{0:T(1024)(128)(4,1)S(1)}, s32[]{:S(2)}) async-start(s8[4239360]{0:T(1024)(128)(4,1)} %bitcast.132), calls=%async_computation.7 | async-start | bytes 8388608
  464.9 5.0 copy-start.3
  464.9 96.6 %all-to-all-start.2 = ((bf16[16,80,2880]{2,1,0:T(8,128)(2,1)}), bf16[16,80,2880]{2,1,0:T(8,128)(2,1)}, u32[]{:S(2)}, u32[]{:S(2)}) async-start(bf16[16,80,2880]{2,1,0:T(8,128)(2,1)} %bitcast.116), calls=%async_computation.2 | async-start | bytes 15073280 | tf_op jit(solution)/shard_map/all_to_all | solution.py:134
  594.5 6.1 copy-start.1
  602.1 12.1 %collective-permute-start.1 = (bf16[128,2880]{0,1:T(8,128)(2,1)S(1)}, bf16[128,2880]{0,1:T(8,128)(2,1)S(1)}, u32[]{:S(2)}, u32[]{:S(2)}) collective-permute-start(bf16[128,2880]{0,1:T(8,128)(2,1)S(1)} %add_convert_fusion), channel_id=1, source_target_pairs={{0,16},{16,32},{32,48},{48,64},{64,80},{80,96},{96,112},{112,0},{1... | collective-permute-start | bytes 2211848 | tf_op jit(solution)/shard_map/ppermute | solution.py:21
